TPU v7x, 32 devices: a whole 2x2x4 slice. The times are simulated.
32 devices in a mesh: walker: 2 (over core), slab: 2 (over x), chol: 8 (over z, y).
Axes of the slice: x: 2, y: 2, z: 4, core: 2. Of those that a mesh axis runs over, the one named last changes fastest.
Arguments:
- cholesky_factors: bfloat16 [96, 256, 2048], P('chol', None, 'slab'), may hold values from -0.13183594 to 0.13183594
- greens: bfloat16 [2, 256, 2048], P('walker', 'chol', 'slab'), may hold values from -1.7265625 to 1.7265625
- walker_weights: float32 [2], P('walker'), may hold values from 0.3 to 3
Outputs:
- fock: float32 [256, 2048], P(('walker', 'chol'), 'slab')
All inputs are finite; a program needn't handle non-finite values.
Results may differ from a plain program's by a relative error of at most 0.0029.
Values may be sent and summed in bfloat16 or wider, within the bound.
A program may use at most 64 MiB of HBM per device.

v0:
```python
import functools

import jax
import jax.numpy as jnp
from jax import lax
from jax.experimental import pallas as pl
from jax.experimental.pallas import tpu as pltpu
from jax.sharding import PartitionSpec as P

MESH = pl.DeviceIdType.MESH
NT = (((1,), (1,)), ((), ()))


def exchange_kernel(
    sizes, l_hbm, theta_hbm, weight_ref, out_ref,
    lv, th, wbuf, own, sbuf, rbuf, own_small, sbuf_small, rbuf_small, fsend, frecv, yrecv,
    l_sem, w_sem, z_send, y_send, c_send, th_recv, x_send, x_recv, f_send, f_recv, fy_send, fy_recv,
):
    n_chol, vectors, occupied, block_rows = sizes
    n_hi = n_chol // 2
    half = occupied // 2
    chunk_rows = 2 * block_rows
    n_chunks = n_hi
    n_groups = n_hi // 2
    w = lax.axis_index("walker")
    s = lax.axis_index("slab")
    me = lax.axis_index("chol")
    z, y = me // 2, me % 2
    step = 1 - 2 * (z % 2)
    sibling = {"walker": 1 - w}
    peer = {"slab": 1 - s}
    y_peer = {"chol": z * 2 + 1 - y}

    def partner(t):
        k = n_hi - 1 - t
        return lax.rem(z // 2 + k // 2, n_groups) * 2 + lax.rem(z + k, 2)

    def line(at):
        return jnp.logical_and(at >= 0, at < n_hi)

    def signal(to):
        pl.semaphore_signal(barrier, inc=1, device_id=to, device_id_type=MESH)

    barrier = pltpu.get_barrier_semaphore()
    signal(sibling)
    signal(y_peer)
    signal({"chol": (z + step) * 2 + y})
    signal(peer)

    @pl.when(line(z - step))
    def _():
        signal({"chol": (z - step) * 2 + y})

    mine = pl.ds(pl.multiple_of(w * half, half), half)
    other = pl.ds(pl.multiple_of((1 - w) * half, half), half)
    keep = pltpu.make_async_copy(theta_hbm.at[0], th.at[w, me], l_sem.at[2])
    load_mine = pltpu.make_async_copy(l_hbm.at[:, mine], lv.at[:, mine], l_sem.at[0])
    load_other = pltpu.make_async_copy(l_hbm.at[:, other], lv.at[:, other], l_sem.at[1])
    keep.start()
    wbuf[w] = jnp.full(wbuf.shape[1:], weight_ref[0], jnp.float32)
    keep.wait()

    pl.semaphore_wait(barrier, 4 + line(z - step).astype(jnp.int32))

    def rdma(src, dst, send, recv, to):
        return pltpu.make_async_remote_copy(
            src_ref=src, dst_ref=dst, send_sem=send, recv_sem=recv, device_id=to, device_id_type=MESH
        )

    def pass_on(block, sem, to):
        return rdma(th.at[w, block], th.at[w, block], sem.at[block], th_recv.at[w, block], to)

    def arrived(walker, block):
        rdma(th.at[walker, block], th.at[walker, block], c_send.at[0], th_recv.at[walker, block], sibling).wait_recv()

    def relay(block, onward):
        @pl.when(line(onward))
        def _():
            pass_on(block, z_send, {"chol": onward * 2 + y}).start()

        pass_on(block, y_send, y_peer).start()
        pass_on(block, c_send, sibling).start()

    def from_line(d, way):
        at = z + way * d

        @pl.when(line(at))
        def _():
            arrived(w, at * 2 + y)
            relay(at * 2 + y, z - way)

    def from_y(at):
        @pl.when(line(at))
        def _():
            arrived(w, at * 2 + 1 - y)
            pass_on(at * 2 + 1 - y, c_send, sibling).start()

    @pl.when(line(z - step))
    def _():
        rdma(th.at[w, me], th.at[w, me], z_send.at[n_chol], th_recv.at[w, me], {"chol": (z - step) * 2 + y}).start()

    relay(me, z + step)
    weights = rdma(wbuf.at[w], wbuf.at[w], w_sem.at[0], w_sem.at[1], sibling)
    weights.start()
    load_mine.start()
    load_other.start()
    from_line(1, step)
    from_line(1, -step)
    from_y(z)
    from_y(z + step)
    from_line(2, step)
    from_line(2, -step)

    def slots(unit, q):
        if isinstance(unit, tuple):
            at, to = (unit[1], q), (n_chunks - 1 + unit[1], q)
            bufs = own_small.at[at], sbuf_small.at[at], rbuf_small.at[at]
        else:
            at = to = (unit, q)
            bufs = own.at[at], sbuf.at[at], rbuf.at[at]
        return bufs + (rdma(bufs[1], bufs[2], x_send.at[to], x_recv.at[to], peer),)

    def margins(unit, q):
        if isinstance(unit, tuple):
            count = block_rows
            start = z * chunk_rows + jnp.where(unit[1] == 0, 1 - y, y) * block_rows
        else:
            count = chunk_rows
            start = partner(unit) * chunk_rows
        rows = pl.ds(pl.multiple_of(w * half + start, count), count)
        x = lv[:, rows, :].reshape(vectors * count, -1)
        theta = th[:, pl.ds(4 * q, 4)]
        width = 4 * theta.shape[2]
        both = lax.dot_general(
            x, theta.reshape(2 * width, -1), NT, preferred_element_type=jnp.float32
        )
        a = wbuf[0][:1, :1] * both[:, :width] + wbuf[1][:1, :1] * both[:, width:]
        keep_ref, send_ref, _, copy = slots(unit, q)
        keep_ref[...] = a
        send_ref[...] = a.astype(jnp.bfloat16)
        copy.start()

    def group_arrived(q):
        for k in range(4):
            arrived(1 - w, 4 * q + k)

    def big_margins(q):
        def body(t, carry):
            margins(t, q)
            return carry

        lax.fori_loop(0, n_chunks - 1, body, 0)

    def small_margins(q):
        def body(i, carry):
            margins((None, i), q)
            return carry

        lax.fori_loop(0, 2, body, 0)

    here = z // 2
    group_arrived(here)
    rdma(wbuf.at[1 - w], wbuf.at[1 - w], w_sem.at[0], w_sem.at[1], sibling).wait_recv()
    load_mine.wait()
    big_margins(here)
    for d in range(3, n_hi):
        from_line(d, step)
        from_line(d, -step)
    from_y(z - step)
    for d in range(2, n_hi):
        from_y(z + d * step)
        from_y(z - d * step)
    for k in range(1, n_groups):
        q = lax.rem(here + k, n_groups)
        group_arrived(q)
        big_margins(q)
    for k in range(n_groups):
        small_margins(lax.rem(here + k, n_groups))
    load_other.wait()

    def fock(unit, q):
        keep_ref, _, got_ref, copy = slots(unit, q)
        copy.wait_recv()
        total = keep_ref[...] + got_ref[...].astype(jnp.float32)
        count, width = total.shape[0] // vectors, total.shape[1]
        total = jnp.concatenate(
            [total[g * count : (g + 1) * count] for g in range(vectors)], axis=1
        )
        high = total.astype(jnp.bfloat16)
        low = (total - high.astype(jnp.float32)).astype(jnp.bfloat16)
        m = pl.ds(pl.multiple_of(q * width, width), width)
        both = jnp.dot(
            jnp.concatenate([high, low], axis=0),
            lv[:, m, :].reshape(vectors * width, -1),
            preferred_element_type=jnp.float32,
        )
        return both[:count] + both[count:]

    def to_y(t, d):
        to = {"chol": jnp.where(t == n_chunks - 2, partner(t), z) * 2 + 1 - y}
        return rdma(fsend.at[t, d], yrecv.at[t], fy_send.at[t], fy_recv.at[t], to)

    def along_z(t):
        to = {"chol": partner(t) * 2 + y}
        return rdma(fsend.at[t, y], frecv.at[z], f_send.at[t], f_recv.at[z], to)

    def add_and_pass(t):
        to_y(t, 1 - y).wait_recv()
        fsend[t, y] = fsend[t, y] + yrecv[t]
        along_z(t).start()

    for k in range(n_groups):
        q = lax.rem(here + k, n_groups)
        first, last = k == 0, k == n_groups - 1

        def big(t, carry):
            f = fock(t, q)
            for d in range(2):
                rows = f[d * block_rows : (d + 1) * block_rows]
                fsend[t, d] = rows if first else fsend[t, d] + rows
            if last:
                to_y(t, 1 - y).start()

                @pl.when(t == n_chunks - 2)
                def _():
                    along_z(t).start()

                @pl.when(t > 0)
                def _():
                    add_and_pass(t - 1)

            return carry

        lax.fori_loop(0, n_chunks - 1, big, 0)

    for k in range(n_groups):
        q = lax.rem(here + k, n_groups)
        first, last = k == 0, k == n_groups - 1

        def small(i, carry):
            rows = fock((None, i), q)
            fsend[n_chunks - 1, i] = rows if first else fsend[n_chunks - 1, i] + rows
            if last:

                @pl.when(i == 0)
                def _():
                    to_y(n_chunks - 1, 0).start()

            return carry

        lax.fori_loop(0, 2, small, 0)

    result = fsend[n_chunks - 1, 1]
    for k in range(1, n_hi):
        source = lax.rem(z + k, n_hi)
        rdma(frecv.at[source], frecv.at[source], f_send.at[0], f_recv.at[source], sibling).wait_recv()
        result = result + frecv[source]
    for t in (n_chunks - 2, n_chunks - 1):
        to_y(t, 0).wait_recv()
        result = result + yrecv[t]
    out_ref[...] = result

    weights.wait_send()

    @pl.when(line(z - step))
    def _():
        rdma(th.at[w, me], th.at[w, me], z_send.at[n_chol], th_recv.at[w, me], peer).wait_send()

    pass_on(me, z_send, peer).wait_send()

    def drain_theta(at, carry):
        for d in range(2):
            pass_on(at * 2 + d, c_send, sibling).wait_send()
        pass_on(at * 2 + y, y_send, peer).wait_send()
        onward = jnp.where(at > z, z - 1, z + 1)

        @pl.when(jnp.logical_and(at != z, line(onward)))
        def _():
            pass_on(at * 2 + y, z_send, peer).wait_send()

        return carry

    lax.fori_loop(0, n_hi, drain_theta, 0)

    def drain(t, carry):
        for q in range(n_groups):
            slots(t, q)[3].wait_send()
        to_y(t, 1 - y).wait_send()
        along_z(t).wait_send()
        return carry

    lax.fori_loop(0, n_chunks - 1, drain, 0)
    for i in range(2):
        for q in range(n_groups):
            slots((None, i), q)[3].wait_send()
    to_y(n_chunks - 1, 0).wait_send()


def fused(n_chol, cholesky_factors, greens, walker_weights):
    vectors, occupied, orbitals = cholesky_factors.shape
    theta_rows = greens.shape[1]
    block_rows = occupied // (2 * n_chol)
    n_hi = n_chol // 2
    n_groups = n_hi // 2
    rows = vectors * 2 * block_rows
    width = 4 * theta_rows
    dma = pltpu.SemaphoreType.DMA
    return pl.pallas_call(
        functools.partial(exchange_kernel, (n_chol, vectors, occupied, block_rows)),
        out_shape=jax.ShapeDtypeStruct((block_rows, orbitals), jnp.float32),
        in_specs=[
            pl.BlockSpec(memory_space=pl.ANY),
            pl.BlockSpec(memory_space=pl.ANY),
            pl.BlockSpec(memory_space=pltpu.SMEM),
        ],
        out_specs=pl.BlockSpec(memory_space=pltpu.VMEM),
        scratch_shapes=[
            pltpu.VMEM((vectors, occupied, orbitals), jnp.bfloat16),
            pltpu.VMEM((2, n_chol, theta_rows, orbitals), jnp.bfloat16),
            pltpu.VMEM((2, 8, 128), jnp.float32),
            pltpu.VMEM((n_hi - 1, n_groups, rows, width), jnp.float32),
            pltpu.VMEM((n_hi - 1, n_groups, rows, width), jnp.bfloat16),
            pltpu.VMEM((n_hi - 1, n_groups, rows, width), jnp.bfloat16),
            pltpu.VMEM((2, n_groups, rows // 2, width), jnp.float32),
            pltpu.VMEM((2, n_groups, rows // 2, width), jnp.bfloat16),
            pltpu.VMEM((2, n_groups, rows // 2, width), jnp.bfloat16),
            pltpu.VMEM((n_hi, 2, block_rows, orbitals), jnp.float32),
            pltpu.VMEM((n_hi, block_rows, orbitals), jnp.float32),
            pltpu.VMEM((n_hi, block_rows, orbitals), jnp.float32),
            dma((3,)),
            dma((2,)),
            dma((n_chol + 1,)),
            dma((n_chol,)),
            dma((n_chol,)),
            dma((2, n_chol)),
            dma((n_hi + 1, n_groups)),
            dma((n_hi + 1, n_groups)),
            dma((n_hi,)),
            dma((n_hi,)),
            dma((n_hi,)),
            dma((n_hi,)),
        ],
        compiler_params=pltpu.CompilerParams(collective_id=0, has_side_effects=True),
    )(cholesky_factors, greens, walker_weights)


def plain(cholesky_factors, greens, walker_weights):
    panel_sum_terms = jnp.einsum(
        "gnp,mp->gnm",
        cholesky_factors,
        lax.all_gather(greens[0], "chol", axis=0, tiled=True),
        preferred_element_type=jnp.float32,
    )
    margin = lax.psum(panel_sum_terms, "slab").astype(jnp.bfloat16)
    terms = jnp.einsum("gnm,gmp->np", margin, cholesky_factors, preferred_element_type=jnp.float32)
    weighted = walker_weights[0] * terms
    return lax.psum_scatter(weighted, ("walker", "chol"), scatter_dimension=0, tiled=True)


def solution(mesh):
    walkers, slabs, n_chol = (mesh.shape[axis] for axis in ("walker", "slab", "chol"))

    def per_device(cholesky_factors, greens, walker_weights):
        occupied = cholesky_factors.shape[1]
        pair = walkers == 2 and slabs == 2 and greens.shape[0] == 1
        fits = n_chol % 4 == 0 and occupied % (16 * n_chol) == 0 and 4 * greens.shape[1] % 128 == 0
        if pair and fits:
            return fused(n_chol, cholesky_factors, greens, walker_weights)
        return plain(cholesky_factors, greens, walker_weights)

    in_specs = (P("chol", None, "slab"), P("walker", "chol", "slab"), P("walker"))
    out_specs = P(("walker", "chol"), "slab")
    return jax.shard_map(
        per_device, mesh=mesh, in_specs=in_specs, out_specs=out_specs, check_vma=False
    )
```

profile of v0, /device:TPU:0, one launch (start us, length us, event | category | flops | bytes accessed | tf_op | source)
XLA Modules:
  0.0 38.5 jit_solution(7473421951872927667)
XLA Ops:
  0.7 36.4 %shard_map.37 = f32[16,1024]{1,0:T(8,128)} custom-call(bf16[12,256,1024]{2,1,0:T(8,128)(2,1)} %l_hbm.1, bf16[1,32,1024]{2,1,0:T(8,128)(2,1)} %theta_hbm.1, f32[1]{0:T(128)S(6)} %copy.5.weight_ref), custom_call_target="tpu_custom_call" | custom-call | tf_op jit(solution)/shard_map/pallas_call | solution.py:308
  37.1 1.5 %copy.6 = f32[16,1024]{1,0:T(8,128)} copy(f32[16,1024]{1,0:T(8,128)} %shard_map.37) | data formatting | bytes 131072
where the time goes:
time: 38.7 us; the launch traced here: 38.5 us
  Pallas kernels  36.4 us (94%)
  local copies, waits for them, and re-layouts  1.47 us (4%)
  between operations  0.66 us (2%)
    pallas_call x1, Pallas kernels, fused(): pl.pallas_call(functools.partial(exchange_kernel, (n_chol, vectors, occup...  36.4 us
    unnamed x1, local copies, waits for them, and re-layouts  1.47 us

commit v1 on v0

v1 whole, which is shorter than its diff:
```python
import functools

import jax
import jax.numpy as jnp
from jax import lax
from jax.experimental import pallas as pl
from jax.experimental.pallas import tpu as pltpu
from jax.sharding import PartitionSpec as P

MESH = pl.DeviceIdType.MESH
NT = (((1,), (1,)), ((), ()))
VMEM_LIMIT = 56000000


def exchange_kernel(
    sizes, l_hbm, theta_hbm, weight_ref, out_ref,
    lv, raw, th, wbuf, own, sbuf, rbuf, facc, yrecv, frecv, nrecv,
    l_sem, w_send, w_recv, raw_send, raw_recv, th_send, th_recv, c_send, c_recv,
    x_send, x_recv, fy_send, fy_recv, f_send, f_recv, n_send, n_recv, seen,
):
    n_chol, vectors, occupied, block_rows = sizes
    n_hi = n_chol // 2
    half = occupied // 2
    chunk_rows = 2 * block_rows
    theta_rows = 2 * block_rows
    n_groups = n_hi // 2
    last = n_hi - 1
    w = lax.axis_index("walker")
    s = lax.axis_index("slab")
    me = lax.axis_index("chol")
    z, y = me // 2, me % 2
    zn = z + 1 - 2 * (z % 2)
    sibling = {"walker": 1 - w}
    peer = {"slab": 1 - s}

    def chol(at, col):
        return {"chol": at * 2 + col}

    def partner(t):
        k = n_hi - 1 - t
        return lax.rem(z // 2 + k // 2, n_groups) * 2 + lax.rem(z + k, 2)

    def line(at):
        return jnp.logical_and(at >= 0, at < n_hi)

    def signal(sem, to):
        pl.semaphore_signal(sem, inc=1, device_id=to, device_id_type=MESH)

    def rdma(src, dst, send, recv, to):
        return pltpu.make_async_remote_copy(
            src_ref=src, dst_ref=dst, send_sem=send, recv_sem=recv, device_id=to, device_id_type=MESH
        )

    barrier = pltpu.get_barrier_semaphore()
    signal(barrier, sibling)
    signal(barrier, peer)
    signal(barrier, chol(z, 1 - y))
    for way in (-1, 1):

        @pl.when(line(z + way))
        def _():
            signal(barrier, chol(z + way, y))

    mine = pl.ds(pl.multiple_of(w * half, half), half)
    other = pl.ds(pl.multiple_of((1 - w) * half, half), half)
    keep = pltpu.make_async_copy(theta_hbm.at[0], raw.at[w], l_sem.at[2])
    load_mine = pltpu.make_async_copy(l_hbm.at[:, mine], lv.at[:, mine], l_sem.at[0])
    load_other = pltpu.make_async_copy(l_hbm.at[:, other], lv.at[:, other], l_sem.at[1])
    keep.start()
    load_mine.start()
    load_other.start()
    wbuf[w] = jnp.full(wbuf.shape[1:], weight_ref[0], jnp.float32)
    keep.wait()
    near = line(z - 1).astype(jnp.int32) + line(z + 1).astype(jnp.int32)
    pl.semaphore_wait(barrier, 3 + near)

    def give(walker):
        return rdma(raw.at[walker], raw.at[walker], raw_send, raw_recv, sibling)

    def give_weight(walker):
        return rdma(wbuf.at[walker], wbuf.at[walker], w_send, w_recv, sibling)

    give(w).start()
    give_weight(w).start()

    def vouch(stage, along_line):
        signal(seen.at[stage, 2], chol(z, 1 - y))
        if along_line:
            for d, way in enumerate((-1, 1)):

                @pl.when(line(z + way))
                def _():
                    signal(seen.at[stage, 1 - d], chol(z + way, y))

    def vouched(stage, along_line):
        pl.semaphore_wait(seen.at[stage, 2], 1)
        if along_line:
            for d, way in enumerate((-1, 1)):

                @pl.when(line(z + way))
                def _():
                    pl.semaphore_wait(seen.at[stage, d], 1)

    def spread(at, col):
        to = at * 2 + col
        return rdma(th.at[me, w], th.at[me, w], th_send.at[to], th_recv.at[me], {"chol": to})

    def spread_line(d, col):
        if d < n_hi:
            for way in (-1, 1):

                @pl.when(line(z + way * d))
                def _():
                    spread(z + way * d, col).start()

    vouch(0, True)
    give(1 - w).wait_recv()
    give_weight(1 - w).wait_recv()
    combined = wbuf[0][:1, :1] * raw[0].astype(jnp.float32) + wbuf[1][:1, :1] * raw[1].astype(jnp.float32)
    th[me] = combined.astype(jnp.bfloat16).reshape(th.shape[1:])
    spread(z, 1 - y).start()
    spread_line(1, y)

    def kind_of(kind):
        if kind == 0:
            return 4, 0, me, 1
        if kind == 1:
            return 4, 1, z * 2 + 1 - y, 1
        if kind == 2:
            return 2, 2, zn * 2, 2
        q = lax.rem(z // 2 + kind - 2, n_groups)
        return 1, 4 * (kind - 2), q * 4, 4

    unit = vectors // 4 * block_rows
    n_kinds = 3 + n_groups - 1

    def place(t, kind, h):
        pack, at, _, _ = kind_of(kind)
        span = pl.ds(at * unit, vectors // pack * block_rows)
        return (t, span) if h is None else (t, h, span)

    def xcopy(t, kind, h):
        if h is None:
            pick = (t, slice(None), place(t, kind, None)[1])
            sem = (t, kind, 0)
        else:
            pick = place(t, kind, h)
            sem = (t, kind, h)
        return rdma(sbuf.at[pick], rbuf.at[pick], x_send.at[sem], x_recv.at[sem], peer)

    def margins(t, kind, zt, h=None):
        pack, _, block, blocks = kind_of(kind)
        halves = (0, 1) if h is None else (h,)
        pieces = []
        for k in halves:
            start = w * half + zt * chunk_rows + k * block_rows
            rows = pl.ds(pl.multiple_of(start, block_rows), block_rows)
            pieces.append(lv[:, rows, :].reshape(vectors * block_rows, -1))
        x = pieces[0] if len(pieces) == 1 else jnp.concatenate(pieces, axis=0)
        theta = th[pl.ds(block, blocks)].reshape(blocks * theta_rows, -1)
        a = lax.dot_general(x, theta, NT, preferred_element_type=jnp.float32)
        per = vectors // pack * block_rows
        for i, k in enumerate(halves):
            parts = [a[(i * pack + p) * per : (i * pack + p + 1) * per] for p in range(pack)]
            packed = parts[0] if pack == 1 else jnp.concatenate(parts, axis=1)
            own[place(t, kind, k)] = packed
            sbuf[place(t, kind, k)] = packed.astype(jnp.bfloat16)
        xcopy(t, kind, h).start()

    def zt_of(t):
        return z if t == last else partner(t)

    load_mine.wait()

    def own_margins(t, carry):
        margins(t, 0, jnp.where(t == last, z, partner(t)))
        return carry

    step = max(1, n_hi // 2)
    lax.fori_loop(0, step, own_margins, 0)
    for stage in range(1, n_hi):
        vouched(stage - 1, stage < n_hi - 1)
        if stage < n_hi - 1:
            vouch(stage, stage < n_hi - 2)
        spread_line(stage + 1, y)
        spread_line(stage, 1 - y)
        if step < n_hi:
            own_margins(step, 0)
            step += 1

    def landed(block):
        rdma(th.at[block, w], th.at[block, w], c_send.at[0], th_recv.at[block], sibling).wait_recv()

    def hand(block):
        return rdma(th.at[block, w], th.at[block, w], c_send.at[block], c_recv.at[block], sibling)

    def relay(block):
        landed(block)
        hand(block).start()

    def handed(block):
        rdma(th.at[block, 1 - w], th.at[block, 1 - w], c_send.at[0], c_recv.at[block], sibling).wait_recv()

    y_block = z * 2 + 1 - y
    relay(y_block)
    relay(zn * 2 + y)
    handed(y_block)

    def y_margins(t, carry):
        margins(t, 1, partner(t))
        return carry

    lax.fori_loop(0, last, y_margins, 0)
    relay(zn * 2 + 1 - y)
    handed(zn * 2 + y)
    handed(zn * 2 + 1 - y)

    def z_margins(t, carry):
        margins(t, 2, partner(t))
        return carry

    lax.fori_loop(0, last - 1, z_margins, 0)
    for kind in range(3, n_kinds):
        q = lax.rem(z // 2 + kind - 2, n_groups)
        for col in (y, 1 - y):
            for k in range(2):
                relay(q * 4 + k * 2 + col)
    for kind in range(3, n_kinds):
        q = lax.rem(z // 2 + kind - 2, n_groups)
        for k in range(4):
            handed(q * 4 + k)

    def far_margins(t, carry):
        for kind in range(3, n_kinds):
            margins(t, kind, partner(t))
        return carry

    lax.fori_loop(0, last - 1, far_margins, 0)
    margins(last - 1, 2, partner(last - 1))
    far_margins(last - 1, 0)

    def small_margins(i, carry):
        h = jnp.where(i == 0, 1 - y, y)
        for kind in range(1, n_kinds):
            margins(last, kind, z, h)
        return carry

    lax.fori_loop(0, 2, small_margins, 0)
    load_other.wait()

    def fock(t, kinds, h=None):
        halves = (0, 1) if h is None else (h,)
        for kind in kinds:
            split = h is not None and kind > 0
            if h is None or split:
                xcopy(t, kind, h).wait_recv()
        lhs = []
        rhs = []
        for kind in kinds:
            pack, _, block, blocks = kind_of(kind)
            count = vectors // pack
            columns = []
            for k in halves:
                at = place(t, kind, k)
                total = own[at] + rbuf[at].astype(jnp.float32)
                columns.append(
                    jnp.concatenate([total[g * block_rows : (g + 1) * block_rows] for g in range(count)], axis=1)
                )
            lhs.append(columns[0] if len(columns) == 1 else jnp.concatenate(columns, axis=0))
            width = blocks * theta_rows
            m = pl.ds(pl.multiple_of(block * theta_rows, theta_rows), width)
            for g in range(count):
                for p in range(pack):
                    rhs.append(lv[p * count + g, m, :])
        total = lhs[0] if len(lhs) == 1 else jnp.concatenate(lhs, axis=1)
        high = total.astype(jnp.bfloat16)
        low = (total - high.astype(jnp.float32)).astype(jnp.bfloat16)
        both = jnp.dot(
            jnp.concatenate([high, low], axis=0),
            jnp.concatenate(rhs, axis=0),
            preferred_element_type=jnp.float32,
        )
        n = len(halves) * block_rows
        return both[:n] + both[n:]

    near_kinds = (0, 1, 2)
    far_kinds = tuple(range(3, n_kinds))

    def near_fock(t, carry):
        f = fock(t, near_kinds)
        for k in range(2):
            facc[t, k] = f[k * block_rows : (k + 1) * block_rows]
        return carry

    def far_fock(t):
        f = fock(t, far_kinds)
        for k in range(2):
            facc[t, k] = facc[t, k] + f[k * block_rows : (k + 1) * block_rows]

    def to_y(t):
        return rdma(facc.at[t, 1 - y], yrecv.at[t], fy_send.at[t], fy_recv.at[t], chol(z, 1 - y))

    def along_z(t):
        return rdma(facc.at[t, y], frecv.at[z], f_send.at[t], f_recv.at[z], chol(partner(t), y))

    def to_next(col):
        return rdma(facc.at[last - 1, col], nrecv.at[y], n_send.at[col], n_recv.at[y], chol(zn, col))

    def add_and_pass(t):
        to_y(t).wait_recv()
        facc[t, y] = facc[t, y] + yrecv[t]
        along_z(t).start()

    lax.fori_loop(0, last - 1, near_fock, 0)

    def far_step(t, carry):
        far_fock(t)
        to_y(t).start()
        return carry

    lax.fori_loop(0, last - 1, far_step, 0)
    near_fock(last - 1, 0)
    far_fock(last - 1)
    to_next(1 - y).start()
    to_next(y).start()
    for t in range(last - 2):
        add_and_pass(t)

    xcopy(last, 0, None).wait_recv()

    def small_fock(i, carry):
        h = jnp.where(i == 0, 1 - y, y)
        facc[last, h] = fock(last, near_kinds, h)
        facc[last, h] = facc[last, h] + fock(last, far_kinds, h)

        @pl.when(i == 0)
        def _():
            to_y(last).start()
            for t in range(max(0, last - 2), last - 1):
                add_and_pass(t)

        return carry

    lax.fori_loop(0, 2, small_fock, 0)

    result = facc[last, y]
    for t in range(last - 1):
        k = n_hi - 1 - t
        source = lax.rem(z // 2 + n_groups - k // 2, n_groups) * 2 + lax.rem(z + k, 2)
        rdma(frecv.at[source], frecv.at[source], f_send.at[0], f_recv.at[source], sibling).wait_recv()
        result = result + frecv[source]
    to_y(last).wait_recv()
    result = result + yrecv[last]
    for col in range(2):
        rdma(nrecv.at[col], nrecv.at[col], n_send.at[0], n_recv.at[col], sibling).wait_recv()
        result = result + nrecv[col]
    out_ref[...] = result

    give(w).wait_send()
    give_weight(w).wait_send()

    def drain_theta(to, carry):
        @pl.when(to != me)
        def _():
            spread(to // 2, to % 2).wait_send()
            hand(to).wait_send()

        return carry

    lax.fori_loop(0, n_chol, drain_theta, 0)

    def drain(t, carry):
        for kind in range(n_kinds):
            xcopy(t, kind, None).wait_send()
        return carry

    lax.fori_loop(0, last, drain, 0)
    xcopy(last, 0, None).wait_send()
    for kind in range(1, n_kinds):
        for h in range(2):
            xcopy(last, kind, h).wait_send()
    for t in range(last - 1):
        to_y(t).wait_send()
        along_z(t).wait_send()
    to_y(last).wait_send()
    for col in range(2):
        to_next(col).wait_send()


def fused(n_chol, cholesky_factors, greens, walker_weights):
    vectors, occupied, orbitals = cholesky_factors.shape
    block_rows = occupied // (2 * n_chol)
    n_hi = n_chol // 2
    n_groups = n_hi // 2
    width = 8 * block_rows
    rows = n_groups * vectors * block_rows
    n_kinds = n_groups + 2
    dma = pltpu.SemaphoreType.DMA
    return pl.pallas_call(
        functools.partial(exchange_kernel, (n_chol, vectors, occupied, block_rows)),
        out_shape=jax.ShapeDtypeStruct((block_rows, orbitals), jnp.float32),
        in_specs=[
            pl.BlockSpec(memory_space=pltpu.HBM),
            pl.BlockSpec(memory_space=pltpu.HBM),
            pl.BlockSpec(memory_space=pltpu.SMEM),
        ],
        out_specs=pl.BlockSpec(memory_space=pltpu.VMEM),
        scratch_shapes=[
            pltpu.VMEM((vectors, occupied, orbitals), jnp.bfloat16),
            pltpu.VMEM((2, 2 * block_rows, orbitals), jnp.bfloat16),
            pltpu.VMEM((n_chol, 2, block_rows, orbitals), jnp.bfloat16),
            pltpu.VMEM((2, 8, 128), jnp.float32),
            pltpu.VMEM((n_hi, 2, rows, width), jnp.float32),
            pltpu.VMEM((n_hi, 2, rows, width), jnp.bfloat16),
            pltpu.VMEM((n_hi, 2, rows, width), jnp.bfloat16),
            pltpu.VMEM((n_hi, 2, block_rows, orbitals), jnp.float32),
            pltpu.VMEM((n_hi, block_rows, orbitals), jnp.float32),
            pltpu.VMEM((n_hi, block_rows, orbitals), jnp.float32),
            pltpu.VMEM((2, block_rows, orbitals), jnp.float32),
            dma((3,)),
            dma,
            dma,
            dma,
            dma,
            dma((n_chol,)),
            dma((n_chol,)),
            dma((n_chol,)),
            dma((n_chol,)),
            dma((n_hi, n_kinds, 2)),
            dma((n_hi, n_kinds, 2)),
            dma((n_hi,)),
            dma((n_hi,)),
            dma((n_hi,)),
            dma((n_hi,)),
            dma((2,)),
            dma((2,)),
            pltpu.SemaphoreType.REGULAR((n_hi, 3)),
        ],
        compiler_params=pltpu.CompilerParams(
            collective_id=0, has_side_effects=True, vmem_limit_bytes=VMEM_LIMIT
        ),
    )(cholesky_factors, greens, walker_weights)


def plain(cholesky_factors, greens, walker_weights):
    panel_sum_terms = jnp.einsum(
        "gnp,mp->gnm",
        cholesky_factors,
        lax.all_gather(greens[0], "chol", axis=0, tiled=True),
        preferred_element_type=jnp.float32,
    )
    margin = lax.psum(panel_sum_terms, "slab").astype(jnp.bfloat16)
    terms = jnp.einsum("gnm,gmp->np", margin, cholesky_factors, preferred_element_type=jnp.float32)
    weighted = walker_weights[0] * terms
    return lax.psum_scatter(weighted, ("walker", "chol"), scatter_dimension=0, tiled=True)


def solution(mesh):
    walkers, slabs, n_chol = (mesh.shape[axis] for axis in ("walker", "slab", "chol"))

    def per_device(cholesky_factors, greens, walker_weights):
        vectors, occupied, _ = cholesky_factors.shape
        pair = walkers == 2 and slabs == 2 and greens.shape[0] == 1
        rows = occupied // n_chol
        fits = n_chol % 4 == 0 and n_chol >= 8 and vectors % 4 == 0 and occupied % (32 * n_chol) == 0 and 4 * rows == 128
        if pair and fits:
            return fused(n_chol, cholesky_factors, greens, walker_weights)
        return plain(cholesky_factors, greens, walker_weights)

    in_specs = (P("chol", None, "slab"), P("walker", "chol", "slab"), P("walker"))
    out_specs = P(("walker", "chol"), "slab")
    return jax.shard_map(
        per_device, mesh=mesh, in_specs=in_specs, out_specs=out_specs, check_vma=False
    )
```

time: 38.7 us -> 37 us (0.956)
  Pallas kernels: 36.4 us -> 34.7 us
    pallas_call x1, Pallas kernels: 36.4 us -> 34.7 us  [fused(): pl.pallas_call(functools.partial(exchange_kernel, (n_chol, vectors, occup...]
    unnamed x1 -> x3, local copies, waits for them, and re-layouts: 1.47 us -> 1.46 us
where the time goes in v1:
time: 37 us; the launch traced here: 36.9 us
  Pallas kernels  34.7 us (94%)
  local copies, waits for them, and re-layouts  1.46 us (4%)
  between operations  0.67 us (2%)
    pallas_call x1, Pallas kernels, fused(): pl.pallas_call(functools.partial(exchange_kernel, (n_chol, vectors, occup...  34.7 us
    unnamed x3, local copies, waits for them, and re-layouts  1.46 us

profile of v1, /device:TPU:0, one launch (start us, length us, event | category | flops | bytes accessed | tf_op | source)
XLA Modules:
  0.0 36.9 jit_solution(3497541566738944044)
XLA Ops:
  0.7 0.0 copy-start
  0.7 0.8 %copy-done = bf16[1,32,1024]{2,1,0:T(8,128)(2,1)S(1)} copy-done((bf16[1,32,1024]{2,1,0:T(8,128)(2,1)S(1)}, bf16[1,32,1024]{2,1,0:T(8,128)(2,1)}, u32[]{:S(2)}) %copy-start) | copy-done | bytes 65560
  1.5 34.7 %shard_map.37 = f32[16,1024]{1,0:T(8,128)S(1)} custom-call(bf16[12,256,1024]{2,1,0:T(8,128)(2,1)} %l_hbm.1, bf16[1,32,1024]{2,1,0:T(8,128)(2,1)S(1)} %copy-done, f32[1]{0:T(128)S(6)} %copy.5.weight_ref), custom_call_target="tpu_custom_call" | custom-call | tf_op jit(solution)/shard_map/pallas_call | solution.py:399
  36.2 0.6 %copy.6 = f32[16,1024]{1,0:T(8,128)} copy(f32[16,1024]{1,0:T(8,128)S(1)} %shard_map.37) | data formatting | bytes 131072
Async XLA Ops:
  0.7 0.8 %copy-start = (bf16[1,32,1024]{2,1,0:T(8,128)(2,1)S(1)}, bf16[1,32,1024]{2,1,0:T(8,128)(2,1)}, u32[]{:S(2)}) copy-start(bf16[1,32,1024]{2,1,0:T(8,128)(2,1)} %theta_hbm.1) | copy-start | bytes 196612

commit v2 on v1

--- a/solution.py
+++ b/solution.py
@@ -170,23 +170,23 @@
     def zt_of(t):
         return z if t == last else partner(t)
 
-    load_mine.wait()
-
-    def own_margins(t, carry):
-        margins(t, 0, jnp.where(t == last, z, partner(t)))
-        return carry
-
-    step = max(1, n_hi // 2)
-    lax.fori_loop(0, step, own_margins, 0)
+    def line_margins(kind):
+        def body(t, carry):
+            margins(t, kind, jnp.where(t == last, z, partner(t)))
+            return carry
+
+        return body
+
     for stage in range(1, n_hi):
         vouched(stage - 1, stage < n_hi - 1)
         if stage < n_hi - 1:
             vouch(stage, stage < n_hi - 2)
         spread_line(stage + 1, y)
         spread_line(stage, 1 - y)
-        if step < n_hi:
-            own_margins(step, 0)
-            step += 1
+        if stage == 1:
+            load_mine.wait()
+        line_margins(0)(stage - 1, 0)
+    lax.fori_loop(last, n_hi, line_margins(0), 0)
 
     def landed(block):
         rdma(th.at[block, w], th.at[block, w], c_send.at[0], th_recv.at[block], sibling).wait_recv()
@@ -206,11 +206,7 @@
     relay(zn * 2 + y)
     handed(y_block)
 
-    def y_margins(t, carry):
-        margins(t, 1, partner(t))
-        return carry
-
-    lax.fori_loop(0, last, y_margins, 0)
+    lax.fori_loop(0, n_hi, line_margins(1), 0)
     relay(zn * 2 + 1 - y)
     handed(zn * 2 + y)
     handed(zn * 2 + 1 - y)
@@ -241,7 +237,7 @@
 
     def small_margins(i, carry):
         h = jnp.where(i == 0, 1 - y, y)
-        for kind in range(1, n_kinds):
+        for kind in range(2, n_kinds):
             margins(last, kind, z, h)
         return carry
 
@@ -251,7 +247,7 @@
     def fock(t, kinds, h=None):
         halves = (0, 1) if h is None else (h,)
         for kind in kinds:
-            split = h is not None and kind > 0
+            split = h is not None and kind > 1
             if h is None or split:
                 xcopy(t, kind, h).wait_recv()
         lhs = []
@@ -303,8 +299,10 @@
     def along_z(t):
         return rdma(facc.at[t, y], frecv.at[z], f_send.at[t], f_recv.at[z], chol(partner(t), y))
 
-    def to_next(col):
-        return rdma(facc.at[last - 1, col], nrecv.at[y], n_send.at[col], n_recv.at[y], chol(zn, col))
+    def direct(i, col):
+        t = (0, last - 1)[i]
+        to = chol(partner(t), col)
+        return rdma(facc.at[t, col], nrecv.at[i, y], n_send.at[i, col], n_recv.at[i, y], to)
 
     def add_and_pass(t):
         to_y(t).wait_recv()
@@ -313,20 +311,25 @@
 
     lax.fori_loop(0, last - 1, near_fock, 0)
 
+    far_fock(0)
+    direct(0, 1 - y).start()
+    direct(0, y).start()
+
     def far_step(t, carry):
         far_fock(t)
         to_y(t).start()
         return carry
 
-    lax.fori_loop(0, last - 1, far_step, 0)
+    lax.fori_loop(1, last - 1, far_step, 0)
     near_fock(last - 1, 0)
     far_fock(last - 1)
-    to_next(1 - y).start()
-    to_next(y).start()
-    for t in range(last - 2):
+    direct(1, 1 - y).start()
+    direct(1, y).start()
+    for t in range(1, last - 1):
         add_and_pass(t)
 
-    xcopy(last, 0, None).wait_recv()
+    for kind in range(2):
+        xcopy(last, kind, None).wait_recv()
 
     def small_fock(i, carry):
         h = jnp.where(i == 0, 1 - y, y)
@@ -336,24 +339,29 @@
         @pl.when(i == 0)
         def _():
             to_y(last).start()
-            for t in range(max(0, last - 2), last - 1):
-                add_and_pass(t)
 
         return carry
 
     lax.fori_loop(0, 2, small_fock, 0)
 
     result = facc[last, y]
-    for t in range(last - 1):
+
+    def take_direct(i):
+        total = 0.0
+        for col in range(2):
+            rdma(nrecv.at[i, col], nrecv.at[i, col], n_send.at[0, 0], n_recv.at[i, col], sibling).wait_recv()
+            total = total + nrecv[i, col]
+        return total
+
+    result = result + take_direct(0)
+    for t in range(1, last - 1):
         k = n_hi - 1 - t
         source = lax.rem(z // 2 + n_groups - k // 2, n_groups) * 2 + lax.rem(z + k, 2)
         rdma(frecv.at[source], frecv.at[source], f_send.at[0], f_recv.at[source], sibling).wait_recv()
         result = result + frecv[source]
     to_y(last).wait_recv()
     result = result + yrecv[last]
-    for col in range(2):
-        rdma(nrecv.at[col], nrecv.at[col], n_send.at[0], n_recv.at[col], sibling).wait_recv()
-        result = result + nrecv[col]
+    result = result + take_direct(1)
     out_ref[...] = result
 
     give(w).wait_send()
@@ -375,16 +383,18 @@
         return carry
 
     lax.fori_loop(0, last, drain, 0)
-    xcopy(last, 0, None).wait_send()
-    for kind in range(1, n_kinds):
+    for kind in range(2):
+        xcopy(last, kind, None).wait_send()
+    for kind in range(2, n_kinds):
         for h in range(2):
             xcopy(last, kind, h).wait_send()
-    for t in range(last - 1):
+    for t in range(1, last - 1):
         to_y(t).wait_send()
         along_z(t).wait_send()
     to_y(last).wait_send()
-    for col in range(2):
-        to_next(col).wait_send()
+    for i in range(2):
+        for col in range(2):
+            direct(i, col).wait_send()
 
 
 def fused(n_chol, cholesky_factors, greens, walker_weights):
@@ -416,7 +426,7 @@
             pltpu.VMEM((n_hi, 2, block_rows, orbitals), jnp.float32),
             pltpu.VMEM((n_hi, block_rows, orbitals), jnp.float32),
             pltpu.VMEM((n_hi, block_rows, orbitals), jnp.float32),
-            pltpu.VMEM((2, block_rows, orbitals), jnp.float32),
+            pltpu.VMEM((2, 2, block_rows, orbitals), jnp.float32),
             dma((3,)),
             dma,
             dma,
@@ -432,8 +442,8 @@
             dma((n_hi,)),
             dma((n_hi,)),
             dma((n_hi,)),
-            dma((2,)),
-            dma((2,)),
+            dma((2, 2)),
+            dma((2, 2)),
             pltpu.SemaphoreType.REGULAR((n_hi, 3)),
         ],
         compiler_params=pltpu.CompilerParams(

time: 37 us -> 35 us (0.946)
  Pallas kernels: 34.7 us -> 32.7 us
    pallas_call x1, Pallas kernels: 34.7 us -> 32.7 us  [fused(): pl.pallas_call(functools.partial(exchange_kernel, (n_chol, vectors, occup...]
where the time goes in v2:
time: 35 us; the launch traced here: 34.9 us
  Pallas kernels  32.7 us (93%)
  local copies, waits for them, and re-layouts  1.46 us (4%)
  between operations  0.67 us (2%)
    pallas_call x1, Pallas kernels, fused(): pl.pallas_call(functools.partial(exchange_kernel, (n_chol, vectors, occup...  32.7 us
    unnamed x3, local copies, waits for them, and re-layouts  1.46 us

profile of v2, /device:TPU:0, one launch (start us, length us, event | category | flops | bytes accessed | tf_op | source)
XLA Modules:
  0.0 34.9 jit_solution(16294254748391110107)
XLA Ops:
  0.7 0.0 copy-start
  0.7 0.8 %copy-done = bf16[1,32,1024]{2,1,0:T(8,128)(2,1)S(1)} copy-done((bf16[1,32,1024]{2,1,0:T(8,128)(2,1)S(1)}, bf16[1,32,1024]{2,1,0:T(8,128)(2,1)}, u32[]{:S(2)}) %copy-start) | copy-done | bytes 65560
  1.5 32.7 %shard_map.37 = f32[16,1024]{1,0:T(8,128)S(1)} custom-call(bf16[12,256,1024]{2,1,0:T(8,128)(2,1)} %l_hbm.1, bf16[1,32,1024]{2,1,0:T(8,128)(2,1)S(1)} %copy-done, f32[1]{0:T(128)S(6)} %copy.5.weight_ref), custom_call_target="tpu_custom_call" | custom-call | tf_op jit(solution)/shard_map/pallas_call | solution.py:409
  34.2 0.6 %copy.6 = f32[16,1024]{1,0:T(8,128)} copy(f32[16,1024]{1,0:T(8,128)S(1)} %shard_map.37) | data formatting | bytes 131072
Async XLA Ops:
  0.7 0.8 %copy-start = (bf16[1,32,1024]{2,1,0:T(8,128)(2,1)S(1)}, bf16[1,32,1024]{2,1,0:T(8,128)(2,1)}, u32[]{:S(2)}) copy-start(bf16[1,32,1024]{2,1,0:T(8,128)(2,1)} %theta_hbm.1) | copy-start | bytes 196612

commit v3 on v1

--- a/solution.py
+++ b/solution.py
@@ -9,13 +9,12 @@
 
 MESH = pl.DeviceIdType.MESH
 NT = (((1,), (1,)), ((), ()))
-VMEM_LIMIT = 56000000
 
 
 def exchange_kernel(
     sizes, l_hbm, theta_hbm, weight_ref, out_ref,
-    lv, raw, th, wbuf, own, sbuf, rbuf, facc, yrecv, frecv, nrecv,
-    l_sem, w_send, w_recv, raw_send, raw_recv, th_send, th_recv, c_send, c_recv,
+    lv, raw, th, rest, wbuf, own, sbuf, rbuf, facc, yrecv, nrecv, bsend, brecv,
+    l_sem, w_send, w_recv, raw_send, raw_recv, rest_send, rest_recv, th_send, th_recv, c_send, c_recv,
     x_send, x_recv, fy_send, fy_recv, f_send, f_recv, n_send, n_recv, seen,
 ):
     n_chol, vectors, occupied, block_rows = sizes
@@ -52,36 +51,26 @@
         )
 
     barrier = pltpu.get_barrier_semaphore()
-    signal(barrier, sibling)
-    signal(barrier, peer)
-    signal(barrier, chol(z, 1 - y))
-    for way in (-1, 1):
-
-        @pl.when(line(z + way))
-        def _():
-            signal(barrier, chol(z + way, y))
+    leads = w == 0
+    signal(barrier, {"slab": 1 - s, "walker": 0})
+
+    @pl.when(leads)
+    def _():
+        signal(barrier, sibling)
+        signal(barrier, chol(z, 1 - y))
+        for way in (-1, 1):
+
+            @pl.when(line(z + way))
+            def _():
+                signal(barrier, chol(z + way, y))
 
     mine = pl.ds(pl.multiple_of(w * half, half), half)
     other = pl.ds(pl.multiple_of((1 - w) * half, half), half)
-    keep = pltpu.make_async_copy(theta_hbm.at[0], raw.at[w], l_sem.at[2])
     load_mine = pltpu.make_async_copy(l_hbm.at[:, mine], lv.at[:, mine], l_sem.at[0])
     load_other = pltpu.make_async_copy(l_hbm.at[:, other], lv.at[:, other], l_sem.at[1])
-    keep.start()
-    load_mine.start()
-    load_other.start()
-    wbuf[w] = jnp.full(wbuf.shape[1:], weight_ref[0], jnp.float32)
-    keep.wait()
-    near = line(z - 1).astype(jnp.int32) + line(z + 1).astype(jnp.int32)
-    pl.semaphore_wait(barrier, 3 + near)
-
-    def give(walker):
-        return rdma(raw.at[walker], raw.at[walker], raw_send, raw_recv, sibling)
-
-    def give_weight(walker):
-        return rdma(wbuf.at[walker], wbuf.at[walker], w_send, w_recv, sibling)
-
-    give(w).start()
-    give_weight(w).start()
+    keep = pltpu.make_async_copy(theta_hbm.at[0], raw.at[0], l_sem.at[2])
+    give = rdma(theta_hbm.at[0], raw.at[1], raw_send, raw_recv, sibling)
+    give_weight = rdma(wbuf.at[1], wbuf.at[1], w_send, w_recv, sibling)
 
     def vouch(stage, along_line):
         signal(seen.at[stage, 2], chol(z, 1 - y))
@@ -103,7 +92,7 @@
 
     def spread(at, col):
         to = at * 2 + col
-        return rdma(th.at[me, w], th.at[me, w], th_send.at[to], th_recv.at[me], {"chol": to})
+        return rdma(th.at[me], th.at[me], th_send.at[to], th_recv.at[me], {"chol": to})
 
     def spread_line(d, col):
         if d < n_hi:
@@ -113,13 +102,57 @@
                 def _():
                     spread(z + way * d, col).start()
 
-    vouch(0, True)
-    give(1 - w).wait_recv()
-    give_weight(1 - w).wait_recv()
-    combined = wbuf[0][:1, :1] * raw[0].astype(jnp.float32) + wbuf[1][:1, :1] * raw[1].astype(jnp.float32)
-    th[me] = combined.astype(jnp.bfloat16).reshape(th.shape[1:])
-    spread(z, 1 - y).start()
-    spread_line(1, y)
+    def hand(block):
+        return rdma(th.at[block], th.at[block], c_send.at[block], c_recv.at[block], sibling)
+
+    hand_rest = rdma(rest, rest, rest_send, rest_recv, sibling)
+
+    def relay(block):
+        rdma(th.at[block], th.at[block], c_send.at[block], th_recv.at[block], sibling).wait_recv()
+        hand(block).start()
+
+    def gather(*blocks):
+        @pl.when(leads)
+        def _():
+            for block in blocks:
+                relay(block)
+
+        @pl.when(jnp.logical_not(leads))
+        def _():
+            for block in blocks:
+                hand(block).wait_recv()
+
+    wbuf[w] = jnp.full(wbuf.shape[1:], weight_ref[0], jnp.float32)
+
+    @pl.when(jnp.logical_not(leads))
+    def _():
+        pl.semaphore_wait(barrier, 1)
+        give.start()
+        give_weight.start()
+        load_mine.start()
+        load_other.start()
+        hand(me).wait_recv()
+        hand_rest.wait_recv()
+
+    @pl.when(leads)
+    def _():
+        keep.start()
+        load_mine.start()
+        load_other.start()
+        keep.wait()
+        give.wait_recv()
+        give_weight.wait_recv()
+        combined = wbuf[0][:1, :1] * raw[0].astype(jnp.float32) + wbuf[1][:1, :1] * raw[1].astype(jnp.float32)
+        rounded = combined.astype(jnp.bfloat16)
+        th[me] = rounded
+        rest[...] = (combined - rounded.astype(jnp.float32)).astype(jnp.bfloat16)
+        near = line(z - 1).astype(jnp.int32) + line(z + 1).astype(jnp.int32)
+        pl.semaphore_wait(barrier, 3 + near)
+        vouch(0, True)
+        spread(z, 1 - y).start()
+        spread_line(1, y)
+        hand(me).start()
+        hand_rest.start()
 
     def kind_of(kind):
         if kind == 0:
@@ -158,7 +191,11 @@
             pieces.append(lv[:, rows, :].reshape(vectors * block_rows, -1))
         x = pieces[0] if len(pieces) == 1 else jnp.concatenate(pieces, axis=0)
         theta = th[pl.ds(block, blocks)].reshape(blocks * theta_rows, -1)
+        if kind == 0:
+            theta = jnp.concatenate([theta, rest[...]], axis=0)
         a = lax.dot_general(x, theta, NT, preferred_element_type=jnp.float32)
+        if kind == 0:
+            a = a[:, :theta_rows] + a[:, theta_rows:]
         per = vectors // pack * block_rows
         for i, k in enumerate(halves):
             parts = [a[(i * pack + p) * per : (i * pack + p + 1) * per] for p in range(pack)]
@@ -170,78 +207,63 @@
     def zt_of(t):
         return z if t == last else partner(t)
 
-    load_mine.wait()
-
-    def own_margins(t, carry):
-        margins(t, 0, jnp.where(t == last, z, partner(t)))
-        return carry
-
-    step = max(1, n_hi // 2)
-    lax.fori_loop(0, step, own_margins, 0)
-    for stage in range(1, n_hi):
+    def line_margins(kind):
+        def body(t, carry):
+            margins(t, kind, jnp.where(t == last, z, partner(t)))
+            return carry
+
+        return body
+
+    def vouching(stage):
         vouched(stage - 1, stage < n_hi - 1)
         if stage < n_hi - 1:
             vouch(stage, stage < n_hi - 2)
         spread_line(stage + 1, y)
         spread_line(stage, 1 - y)
-        if step < n_hi:
-            own_margins(step, 0)
-            step += 1
-
-    def landed(block):
-        rdma(th.at[block, w], th.at[block, w], c_send.at[0], th_recv.at[block], sibling).wait_recv()
-
-    def hand(block):
-        return rdma(th.at[block, w], th.at[block, w], c_send.at[block], c_recv.at[block], sibling)
-
-    def relay(block):
-        landed(block)
-        hand(block).start()
-
-    def handed(block):
-        rdma(th.at[block, 1 - w], th.at[block, 1 - w], c_send.at[0], c_recv.at[block], sibling).wait_recv()
-
-    y_block = z * 2 + 1 - y
-    relay(y_block)
-    relay(zn * 2 + y)
-    handed(y_block)
-
-    def y_margins(t, carry):
-        margins(t, 1, partner(t))
-        return carry
-
-    lax.fori_loop(0, last, y_margins, 0)
-    relay(zn * 2 + 1 - y)
-    handed(zn * 2 + y)
-    handed(zn * 2 + 1 - y)
+
+    load_mine.wait()
+    line_margins(0)(0, 0)
+
+    @pl.when(leads)
+    def _():
+        vouching(1)
+
+    lax.fori_loop(1, n_hi, line_margins(0), 0)
+
+    @pl.when(leads)
+    def _():
+        for stage in range(2, last):
+            vouching(stage)
+
+    gather(z * 2 + 1 - y)
+    line_margins(1)(0, 0)
+
+    @pl.when(leads)
+    def _():
+        vouching(last)
+
+    lax.fori_loop(1, n_hi, line_margins(1), 0)
+    gather(zn * 2 + y, zn * 2 + 1 - y)
 
     def z_margins(t, carry):
         margins(t, 2, partner(t))
         return carry
 
-    lax.fori_loop(0, last - 1, z_margins, 0)
+    lax.fori_loop(0, last, z_margins, 0)
     for kind in range(3, n_kinds):
         q = lax.rem(z // 2 + kind - 2, n_groups)
-        for col in (y, 1 - y):
-            for k in range(2):
-                relay(q * 4 + k * 2 + col)
-    for kind in range(3, n_kinds):
-        q = lax.rem(z // 2 + kind - 2, n_groups)
-        for k in range(4):
-            handed(q * 4 + k)
+        gather(*(q * 4 + k * 2 + col for col in (y, 1 - y) for k in range(2)))
 
     def far_margins(t, carry):
         for kind in range(3, n_kinds):
             margins(t, kind, partner(t))
         return carry
 
-    lax.fori_loop(0, last - 1, far_margins, 0)
-    margins(last - 1, 2, partner(last - 1))
-    far_margins(last - 1, 0)
+    lax.fori_loop(0, last, far_margins, 0)
 
     def small_margins(i, carry):
         h = jnp.where(i == 0, 1 - y, y)
-        for kind in range(1, n_kinds):
+        for kind in range(2, n_kinds):
             margins(last, kind, z, h)
         return carry
 
@@ -251,7 +273,7 @@
     def fock(t, kinds, h=None):
         halves = (0, 1) if h is None else (h,)
         for kind in kinds:
-            split = h is not None and kind > 0
+            split = h is not None and kind > 1
             if h is None or split:
                 xcopy(t, kind, h).wait_recv()
         lhs = []
@@ -297,36 +319,31 @@
         for k in range(2):
             facc[t, k] = facc[t, k] + f[k * block_rows : (k + 1) * block_rows]
 
-    def to_y(t):
-        return rdma(facc.at[t, 1 - y], yrecv.at[t], fy_send.at[t], fy_recv.at[t], chol(z, 1 - y))
-
-    def along_z(t):
-        return rdma(facc.at[t, y], frecv.at[z], f_send.at[t], f_recv.at[z], chol(partner(t), y))
-
-    def to_next(col):
+    def to_y():
+        return rdma(facc.at[last, 1 - y], yrecv, fy_send, fy_recv, chol(z, 1 - y))
+
+    def cross(t, col):
+        return rdma(bsend.at[t, col], brecv.at[t, y], f_send.at[t, col], f_recv.at[t, y], chol(partner(t), col))
+
+    def direct(col):
         return rdma(facc.at[last - 1, col], nrecv.at[y], n_send.at[col], n_recv.at[y], chol(zn, col))
 
-    def add_and_pass(t):
-        to_y(t).wait_recv()
-        facc[t, y] = facc[t, y] + yrecv[t]
-        along_z(t).start()
-
-    lax.fori_loop(0, last - 1, near_fock, 0)
+    lax.fori_loop(0, last, near_fock, 0)
 
     def far_step(t, carry):
         far_fock(t)
-        to_y(t).start()
+        bsend[t] = facc[t].astype(jnp.bfloat16)
+        cross(t, 1 - y).start()
+        cross(t, y).start()
         return carry
 
     lax.fori_loop(0, last - 1, far_step, 0)
-    near_fock(last - 1, 0)
     far_fock(last - 1)
-    to_next(1 - y).start()
-    to_next(y).start()
-    for t in range(last - 2):
-        add_and_pass(t)
-
-    xcopy(last, 0, None).wait_recv()
+    direct(1 - y).start()
+    direct(y).start()
+
+    for kind in range(2):
+        xcopy(last, kind, None).wait_recv()
 
     def small_fock(i, carry):
         h = jnp.where(i == 0, 1 - y, y)
@@ -335,39 +352,43 @@
 
         @pl.when(i == 0)
         def _():
-            to_y(last).start()
-            for t in range(max(0, last - 2), last - 1):
-                add_and_pass(t)
+            to_y().start()
 
         return carry
 
     lax.fori_loop(0, 2, small_fock, 0)
 
     result = facc[last, y]
+
     for t in range(last - 1):
-        k = n_hi - 1 - t
-        source = lax.rem(z // 2 + n_groups - k // 2, n_groups) * 2 + lax.rem(z + k, 2)
-        rdma(frecv.at[source], frecv.at[source], f_send.at[0], f_recv.at[source], sibling).wait_recv()
-        result = result + frecv[source]
-    to_y(last).wait_recv()
-    result = result + yrecv[last]
+        for col in range(2):
+            rdma(brecv.at[t, col], brecv.at[t, col], f_send.at[0, 0], f_recv.at[t, col], sibling).wait_recv()
+            result = result + brecv[t, col].astype(jnp.float32)
+    to_y().wait_recv()
+    result = result + yrecv[...]
     for col in range(2):
         rdma(nrecv.at[col], nrecv.at[col], n_send.at[0], n_recv.at[col], sibling).wait_recv()
         result = result + nrecv[col]
     out_ref[...] = result
 
-    give(w).wait_send()
-    give_weight(w).wait_send()
-
-    def drain_theta(to, carry):
-        @pl.when(to != me)
-        def _():
-            spread(to // 2, to % 2).wait_send()
+    @pl.when(jnp.logical_not(leads))
+    def _():
+        give.wait_send()
+        give_weight.wait_send()
+
+    @pl.when(leads)
+    def _():
+        def drain_theta(to, carry):
             hand(to).wait_send()
 
-        return carry
-
-    lax.fori_loop(0, n_chol, drain_theta, 0)
+            @pl.when(to != me)
+            def _():
+                spread(to // 2, to % 2).wait_send()
+
+            return carry
+
+        lax.fori_loop(0, n_chol, drain_theta, 0)
+        hand_rest.wait_send()
 
     def drain(t, carry):
         for kind in range(n_kinds):
@@ -375,16 +396,16 @@
         return carry
 
     lax.fori_loop(0, last, drain, 0)
-    xcopy(last, 0, None).wait_send()
-    for kind in range(1, n_kinds):
+    for kind in range(2):
+        xcopy(last, kind, None).wait_send()
+    for kind in range(2, n_kinds):
         for h in range(2):
             xcopy(last, kind, h).wait_send()
-    for t in range(last - 1):
-        to_y(t).wait_send()
-        along_z(t).wait_send()
-    to_y(last).wait_send()
+    to_y().wait_send()
     for col in range(2):
-        to_next(col).wait_send()
+        for t in range(last - 1):
+            cross(t, col).wait_send()
+        direct(col).wait_send()
 
 
 def fused(n_chol, cholesky_factors, greens, walker_weights):
@@ -398,7 +419,7 @@
     dma = pltpu.SemaphoreType.DMA
     return pl.pallas_call(
         functools.partial(exchange_kernel, (n_chol, vectors, occupied, block_rows)),
-        out_shape=jax.ShapeDtypeStruct((block_rows, orbitals), jnp.float32),
+        out_shape=pltpu.VMEM((block_rows, orbitals), jnp.float32),
         in_specs=[
             pl.BlockSpec(memory_space=pltpu.HBM),
             pl.BlockSpec(memory_space=pltpu.HBM),
@@ -408,16 +429,20 @@
         scratch_shapes=[
             pltpu.VMEM((vectors, occupied, orbitals), jnp.bfloat16),
             pltpu.VMEM((2, 2 * block_rows, orbitals), jnp.bfloat16),
-            pltpu.VMEM((n_chol, 2, block_rows, orbitals), jnp.bfloat16),
+            pltpu.VMEM((n_chol, 2 * block_rows, orbitals), jnp.bfloat16),
+            pltpu.VMEM((2 * block_rows, orbitals), jnp.bfloat16),
             pltpu.VMEM((2, 8, 128), jnp.float32),
             pltpu.VMEM((n_hi, 2, rows, width), jnp.float32),
             pltpu.VMEM((n_hi, 2, rows, width), jnp.bfloat16),
             pltpu.VMEM((n_hi, 2, rows, width), jnp.bfloat16),
             pltpu.VMEM((n_hi, 2, block_rows, orbitals), jnp.float32),
-            pltpu.VMEM((n_hi, block_rows, orbitals), jnp.float32),
-            pltpu.VMEM((n_hi, block_rows, orbitals), jnp.float32),
+            pltpu.VMEM((block_rows, orbitals), jnp.float32),
             pltpu.VMEM((2, block_rows, orbitals), jnp.float32),
+            pltpu.VMEM((n_hi - 2, 2, block_rows, orbitals), jnp.bfloat16),
+            pltpu.VMEM((n_hi - 2, 2, block_rows, orbitals), jnp.bfloat16),
             dma((3,)),
+            dma,
+            dma,
             dma,
             dma,
             dma,
@@ -428,16 +453,16 @@
             dma((n_chol,)),
             dma((n_hi, n_kinds, 2)),
             dma((n_hi, n_kinds, 2)),
-            dma((n_hi,)),
-            dma((n_hi,)),
-            dma((n_hi,)),
-            dma((n_hi,)),
+            dma,
+            dma,
+            dma((n_hi - 2, 2)),
+            dma((n_hi - 2, 2)),
             dma((2,)),
             dma((2,)),
             pltpu.SemaphoreType.REGULAR((n_hi, 3)),
         ],
         compiler_params=pltpu.CompilerParams(
-            collective_id=0, has_side_effects=True, vmem_limit_bytes=VMEM_LIMIT
+            collective_id=0, has_side_effects=True
         ),
     )(cholesky_factors, greens, walker_weights)
 

time: 37 us -> 31.9 us (0.86)
  Pallas kernels: 34.7 us -> 30.5 us
  local copies, waits for them, and re-layouts: 1.46 us -> 0.63 us
    pallas_call x1, Pallas kernels: 34.7 us -> 30.5 us  [fused(): pl.pallas_call(functools.partial(exchange_kernel, (n_chol, vectors, occup...]
    unnamed x3 -> x1, local copies, waits for them, and re-layouts: 1.46 us -> 0.63 us
where the time goes in v3:
time: 31.9 us; the launch traced here: 31.8 us
  Pallas kernels  30.5 us (96%)
  between operations  0.66 us (2%)
  local copies, waits for them, and re-layouts  0.63 us (2%)
    pallas_call x1, Pallas kernels, fused(): pl.pallas_call(functools.partial(exchange_kernel, (n_chol, vectors, occup...  30.5 us

profile of v3, /device:TPU:0, one launch (start us, length us, event | category | flops | bytes accessed | tf_op | source)
XLA Modules:
  0.0 31.8 jit_solution(3896334148024723319)
XLA Ops:
  0.7 30.5 %shard_map.37 = f32[16,1024]{1,0:T(8,128)S(1)} custom-call(bf16[12,256,1024]{2,1,0:T(8,128)(2,1)} %l_hbm.1, bf16[1,32,1024]{2,1,0:T(8,128)(2,1)} %theta_hbm.1, f32[1]{0:T(128)S(6)} %copy.6.weight_ref), custom_call_target="tpu_custom_call" | custom-call | tf_op jit(solution)/shard_map/pallas_call | solution.py:420
  31.1 0.6 %copy.5 = f32[16,1024]{1,0:T(8,128)} copy(f32[16,1024]{1,0:T(8,128)S(1)} %shard_map.37) | data formatting | bytes 131072

commit v4 on v3

--- a/solution.py
+++ b/solution.py
@@ -259,7 +259,10 @@
             margins(t, kind, partner(t))
         return carry
 
-    lax.fori_loop(0, last, far_margins, 0)
+    def far_turn(i, carry):
+        return far_margins(jnp.where(i == 0, 0, last - i), carry)
+
+    lax.fori_loop(0, last, far_turn, 0)
 
     def small_margins(i, carry):
         h = jnp.where(i == 0, 1 - y, y)
@@ -337,10 +340,11 @@
         cross(t, y).start()
         return carry
 
-    lax.fori_loop(0, last - 1, far_step, 0)
+    far_step(0, 0)
     far_fock(last - 1)
     direct(1 - y).start()
     direct(y).start()
+    lax.fori_loop(1, last - 1, far_step, 0)
 
     for kind in range(2):
         xcopy(last, kind, None).wait_recv()

time: 31.9 us -> 31.8 us (level)
  no operation moved by 1% of the time
where the time goes in v4:
time: 31.8 us; the launch traced here: 31.7 us
  Pallas kernels  30.4 us (96%)
  between operations  0.66 us (2%)
  local copies, waits for them, and re-layouts  0.63 us (2%)
    pallas_call x1, Pallas kernels, fused(): pl.pallas_call(functools.partial(exchange_kernel, (n_chol, vectors, occup...  30.4 us

profile of v4, /device:TPU:0, one launch (start us, length us, event | category | flops | bytes accessed | tf_op | source)
XLA Modules:
  0.0 31.7 jit_solution(3779963679752871351)
XLA Ops:
  0.7 30.4 %shard_map.37 = f32[16,1024]{1,0:T(8,128)S(1)} custom-call(bf16[12,256,1024]{2,1,0:T(8,128)(2,1)} %l_hbm.1, bf16[1,32,1024]{2,1,0:T(8,128)(2,1)} %theta_hbm.1, f32[1]{0:T(128)S(6)} %copy.6.weight_ref), custom_call_target="tpu_custom_call" | custom-call | tf_op jit(solution)/shard_map/pallas_call | solution.py:424
  31.0 0.6 %copy.5 = f32[16,1024]{1,0:T(8,128)} copy(f32[16,1024]{1,0:T(8,128)S(1)} %shard_map.37) | data formatting | bytes 131072

commit v5 on v4

--- a/solution.py
+++ b/solution.py
@@ -148,9 +148,9 @@
         rest[...] = (combined - rounded.astype(jnp.float32)).astype(jnp.bfloat16)
         near = line(z - 1).astype(jnp.int32) + line(z + 1).astype(jnp.int32)
         pl.semaphore_wait(barrier, 3 + near)
-        vouch(0, True)
         spread(z, 1 - y).start()
         spread_line(1, y)
+        vouch(0, True)
         hand(me).start()
         hand_rest.start()
 
@@ -235,7 +235,17 @@
         for stage in range(2, last):
             vouching(stage)
 
-    gather(z * 2 + 1 - y)
+    early = zn * 2 + y
+
+    @pl.when(leads)
+    def _():
+        relay(z * 2 + 1 - y)
+        relay(early)
+
+    @pl.when(jnp.logical_not(leads))
+    def _():
+        hand(z * 2 + 1 - y).wait_recv()
+
     line_margins(1)(0, 0)
 
     @pl.when(leads)
@@ -243,7 +253,12 @@
         vouching(last)
 
     lax.fori_loop(1, n_hi, line_margins(1), 0)
-    gather(zn * 2 + y, zn * 2 + 1 - y)
+    gather(zn * 2 + 1 - y)
+
+    @pl.when(jnp.logical_not(leads))
+    def _():
+        hand(early).wait_recv()
+
 
     def z_margins(t, carry):
         margins(t, 2, partner(t))
@@ -273,9 +288,12 @@
     lax.fori_loop(0, 2, small_margins, 0)
     load_other.wait()
 
-    def fock(t, kinds, h=None):
+    span = lv.shape[2] // 2
+
+    def fock(t, kinds, h=None, c=None):
         halves = (0, 1) if h is None else (h,)
-        for kind in kinds:
+        cols = slice(None) if c is None else slice(c * span, (c + 1) * span)
+        for kind in kinds if c != 1 else ():
             split = h is not None and kind > 1
             if h is None or split:
                 xcopy(t, kind, h).wait_recv()
@@ -296,7 +314,7 @@
             m = pl.ds(pl.multiple_of(block * theta_rows, theta_rows), width)
             for g in range(count):
                 for p in range(pack):
-                    rhs.append(lv[p * count + g, m, :])
+                    rhs.append(lv[p * count + g, m, cols])
         total = lhs[0] if len(lhs) == 1 else jnp.concatenate(lhs, axis=1)
         high = total.astype(jnp.bfloat16)
         low = (total - high.astype(jnp.float32)).astype(jnp.bfloat16)
@@ -322,8 +340,9 @@
         for k in range(2):
             facc[t, k] = facc[t, k] + f[k * block_rows : (k + 1) * block_rows]
 
-    def to_y():
-        return rdma(facc.at[last, 1 - y], yrecv, fy_send, fy_recv, chol(z, 1 - y))
+    def to_y(c):
+        cols = slice(c * span, (c + 1) * span)
+        return rdma(facc.at[last, 1 - y, :, cols], yrecv.at[:, cols], fy_send.at[c], fy_recv.at[c], chol(z, 1 - y))
 
     def cross(t, col):
         return rdma(bsend.at[t, col], brecv.at[t, y], f_send.at[t, col], f_recv.at[t, y], chol(partner(t), col))
@@ -352,11 +371,13 @@
     def small_fock(i, carry):
         h = jnp.where(i == 0, 1 - y, y)
         facc[last, h] = fock(last, near_kinds, h)
-        facc[last, h] = facc[last, h] + fock(last, far_kinds, h)
-
-        @pl.when(i == 0)
-        def _():
-            to_y().start()
+        for c in range(2):
+            cols = slice(c * span, (c + 1) * span)
+            facc[last, h, :, cols] = facc[last, h, :, cols] + fock(last, far_kinds, h, c)
+
+            @pl.when(i == 0)
+            def _():
+                to_y(c).start()
 
         return carry
 
@@ -368,7 +389,8 @@
         for col in range(2):
             rdma(brecv.at[t, col], brecv.at[t, col], f_send.at[0, 0], f_recv.at[t, col], sibling).wait_recv()
             result = result + brecv[t, col].astype(jnp.float32)
-    to_y().wait_recv()
+    for c in range(2):
+        to_y(c).wait_recv()
     result = result + yrecv[...]
     for col in range(2):
         rdma(nrecv.at[col], nrecv.at[col], n_send.at[0], n_recv.at[col], sibling).wait_recv()
@@ -405,7 +427,8 @@
     for kind in range(2, n_kinds):
         for h in range(2):
             xcopy(last, kind, h).wait_send()
-    to_y().wait_send()
+    for c in range(2):
+        to_y(c).wait_send()
     for col in range(2):
         for t in range(last - 1):
             cross(t, col).wait_send()
@@ -457,8 +480,8 @@
             dma((n_chol,)),
             dma((n_hi, n_kinds, 2)),
             dma((n_hi, n_kinds, 2)),
-            dma,
-            dma,
+            dma((2,)),
+            dma((2,)),
             dma((n_hi - 2, 2)),
             dma((n_hi - 2, 2)),
             dma((2,)),

time: 31.8 us -> 31.9 us (level)
  no operation moved by 1% of the time
where the time goes in v5:
time: 31.9 us; the launch traced here: 31.6 us
  Pallas kernels  30.3 us (95%)
  between operations  0.66 us (2%)
  local copies, waits for them, and re-layouts  0.63 us (2%)
    pallas_call x1, Pallas kernels, fused(): pl.pallas_call(functools.partial(exchange_kernel, (n_chol, vectors, occup...  30.3 us

profile of v5, /device:TPU:0, one launch (start us, length us, event | category | flops | bytes accessed | tf_op | source)
XLA Modules:
  0.0 31.6 jit_solution(9372366053941214172)
XLA Ops:
  0.7 30.3 %shard_map.37 = f32[16,1024]{1,0:T(8,128)S(1)} custom-call(bf16[12,256,1024]{2,1,0:T(8,128)(2,1)} %l_hbm.1, bf16[1,32,1024]{2,1,0:T(8,128)(2,1)} %theta_hbm.1, f32[1]{0:T(128)S(6)} %copy.6.weight_ref), custom_call_target="tpu_custom_call" | custom-call | tf_op jit(solution)/shard_map/pallas_call | solution.py:447
  31.0 0.6 %copy.5 = f32[16,1024]{1,0:T(8,128)} copy(f32[16,1024]{1,0:T(8,128)S(1)} %shard_map.37) | data formatting | bytes 131072
